TPU v7x, 256 devices: a whole 4x4x8 slice. The times are simulated.
256 devices in a mesh: panel: 4 (over x), front: 64 (over y, z, core).
Axes of the slice: x: 4, y: 4, z: 8, core: 2. Of those that a mesh axis runs over, the one named last changes fastest.
Arguments:
- top_source: bfloat16 [4, 128, 4096], P('panel', None, 'front'), may hold values from -6 to 6
- leaf_source: bfloat16 [4, 128, 589824], P('panel', None, 'front'), may hold values from -6 to 6
- top_inverse: bfloat16 [4, 4096, 4096], P('panel', 'front'), may hold values from -1 to 4
- leaf_inverse: bfloat16 [4, 2304, 256, 256], P('panel', 'front'), may hold values from -1 to 4
- boundary: bfloat16 [4, 2304, 128, 256], P('panel', 'front'), may hold values from -0.09375 to 0.09375
- touch_rows: int32 [4, 2304, 128], P('panel', 'front'), may hold values from 0 to 4095, as said below
- coupling: float32 [4, 4096], P('panel', 'front'), may hold values from 0.3 to 1
Outputs:
- top_field: bfloat16 [4, 128, 4096], P('panel', None, 'front')
- leaf_field: bfloat16 [4, 128, 589824], P('panel', None, 'front')
Inputs may be any that keep to these rules, and one draw needn't show every extreme that they name: `touch_rows`: front index d owns top front rows d * 64 to (d + 1) * 64 - 1; leaf j of a panel touches only rows owned by front indices j // 36 - 1, j // 36 and j // 36 + 1.
All inputs are finite; a program needn't handle non-finite values.
Results may differ from a plain program's by a relative error of at most 0.02.
Values may be sent and summed in bfloat16 or wider, within the bound.
A program may use at most 64 MiB of HBM per device.

v0:
```python
import jax
import jax.numpy as jnp
from jax import lax
from jax.sharding import PartitionSpec as P


def extended(value, sides, width):
    for axis, dim in sides:
        devices, length = (lax.axis_size(axis), value.shape[dim])
        up = [(i, (i + 1) % devices) for i in range(devices - 1)]
        down = [(j, i) for i, j in up]
        last = lax.slice_in_dim(value, length - width, length, axis=dim)
        leading = lax.slice_in_dim(value, 0, width, axis=dim)
        before = lax.ppermute(last, axis, up)
        after = lax.ppermute(leading, axis, down)
        value = jnp.concatenate([before, value, after], axis=dim)
    return value


def passed_along(block, axis, distance):
    devices = range(lax.axis_size(axis))
    route = [(i - distance, i) for i in devices if i - distance in devices]
    return lax.ppermute(block, axis, route)


def leaf_apply(inverse_blocks, vectors):
    return jnp.einsum("jab,sjb->sja", inverse_blocks, vectors, preferred_element_type=jnp.float32)


def top_fold(vectors, inverse_rows):
    return lax.dot_general(
        lax.all_gather(vectors, "front", axis=1, tiled=True),
        inverse_rows,
        (((1,), (1,)), ((), ())),
        preferred_element_type=jnp.float32,
    )


def lift_through(values, local_rows, boundary, leaf_inverse):
    rows_here = values.shape[2]
    window = extended(values, (("front", 2),), rows_here)
    flat_rows = local_rows[0].reshape(-1)
    picked = jnp.take(window[0], flat_rows, axis=1).reshape(
        values.shape[1], local_rows.shape[1], local_rows.shape[2]
    )
    lifted = jnp.einsum(
        "jkb,sjk->sjb", boundary[0], picked, preferred_element_type=jnp.float32
    ).astype(jnp.bfloat16)
    results = [leaf_apply(leaf_inverse[0], lifted)]
    return jnp.stack(results)


def place_wave(finished, fresh, first_row, in_range):
    older = lax.dynamic_slice_in_dim(finished, first_row, fresh.shape[1], 1)
    return lax.dynamic_update_slice_in_dim(
        finished, jnp.where(in_range, fresh, older), first_row, 1
    )


def body(top_source, leaf_source, top_inverse, leaf_inverse, boundary, touch_rows, coupling):
    panels_here = top_source.shape[0]
    sources_all = top_source.shape[1]
    rows_here = top_source.shape[2]
    leaf_count = leaf_inverse.shape[1]
    leaf_size = leaf_inverse.shape[2]
    group_count = lax.axis_size("panel")
    group_rank = lax.axis_index("panel")
    row_offset = lax.axis_index("front") * rows_here
    local_rows = touch_rows - (row_offset - rows_here)
    vectors = leaf_source.reshape(panels_here, sources_all, leaf_count, leaf_size)
    panel_index = 0
    interior_one = leaf_apply(leaf_inverse[panel_index], vectors[panel_index]).astype(jnp.bfloat16)
    pushed = jnp.einsum(
        "jkb,sjb->sjk", boundary[panel_index], interior_one, preferred_element_type=jnp.float32
    )
    window_one = jnp.zeros((sources_all, 3 * rows_here), jnp.float32)
    window_one = window_one.at[:, local_rows[panel_index].reshape(-1)].add(
        pushed.reshape(sources_all, -1)
    )
    interior_list = [interior_one]
    window_list = [window_one]
    interior = jnp.stack(interior_list)
    windows = jnp.stack(window_list)
    from_below = passed_along(
        windows[:, :, 2 * rows_here :].astype(jnp.bfloat16), "front", 1
    ).astype(jnp.float32)
    from_above = passed_along(windows[:, :, :rows_here].astype(jnp.bfloat16), "front", -1).astype(
        jnp.float32
    )
    known_part = windows[:, :, rows_here : 2 * rows_here] + from_below + from_above
    wave_count = 1
    wave_rows = sources_all // wave_count
    turn_count = group_count + wave_count - 1

    def forward_turn(turn_index, carry):
        incoming, top_done = carry
        wave_index = turn_index - group_rank
        in_range = (wave_index >= 0) & (wave_index < wave_count)
        first_row = jnp.clip(wave_index, 0, wave_count - 1) * wave_rows
        previous = incoming
        own_terms = top_source[0].astype(jnp.float32) + coupling[0] * previous.astype(jnp.float32)
        solved = top_fold((own_terms - known_part[0]).astype(jnp.bfloat16), top_inverse[0])
        previous = solved.astype(jnp.bfloat16)
        top_parts = [previous]
        top_done = place_wave(top_done, jnp.stack(top_parts), first_row, in_range)
        outgoing = passed_along(previous, "panel", 1)
        return (outgoing, top_done)

    start_edge = jnp.zeros((wave_rows, rows_here), jnp.bfloat16)
    unused_edge, forward_tops = lax.fori_loop(
        0, turn_count, forward_turn, (start_edge, jnp.zeros_like(top_source))
    )

    def backward_turn(turn_index, carry):
        incoming, top_done, fixes_done = carry
        wave_index = turn_index - (group_count - 1 - group_rank)
        in_range = (wave_index >= 0) & (wave_index < wave_count)
        first_row = jnp.clip(wave_index, 0, wave_count - 1) * wave_rows
        arriving = incoming
        top_parts = [None] * panels_here
        fix_parts = [None] * panels_here
        for panel_index in reversed(range(panels_here)):
            correction = top_fold(arriving, top_inverse[panel_index]).astype(jnp.bfloat16)
            top_new = (
                forward_tops[panel_index].astype(jnp.float32) + correction.astype(jnp.float32)
            ).astype(jnp.bfloat16)
            top_parts[panel_index] = top_new
            fix_parts[panel_index] = correction
            arriving = (coupling[panel_index] * top_new.astype(jnp.float32)).astype(jnp.bfloat16)
        top_done = place_wave(top_done, jnp.stack(top_parts), first_row, in_range)
        fixes_done = place_wave(fixes_done, jnp.stack(fix_parts), first_row, in_range)
        outgoing = passed_along(arriving, "panel", -1)
        return (outgoing, top_done, fixes_done)

    backward_state = (start_edge, jnp.zeros_like(top_source), jnp.zeros_like(top_source))
    final_edge, top_field, corrections = lax.fori_loop(0, turn_count, backward_turn, backward_state)
    forward_leaf = (
        interior.astype(jnp.float32)
        - lift_through(forward_tops, local_rows, boundary, leaf_inverse)
    ).astype(jnp.bfloat16)
    leaf_field = (
        forward_leaf.astype(jnp.float32)
        - lift_through(corrections, local_rows, boundary, leaf_inverse)
    ).astype(jnp.bfloat16)
    return (top_field, leaf_field.reshape(panels_here, sources_all, -1))


def solution(mesh):
    placed = (
        P("panel", None, "front"),
        P("panel", None, "front"),
        P("panel", "front", None),
        P("panel", "front", None, None),
        P("panel", "front", None, None),
        P("panel", "front", None),
        P("panel", "front"),
    )
    return jax.shard_map(
        body,
        mesh=mesh,
        in_specs=placed,
        out_specs=(P("panel", None, "front"), P("panel", None, "front")),
        check_vma=False,
    )
```

profile of v0, /device:TPU:1, one launch (start us, length us, event | category | flops | bytes accessed | tf_op | source)
XLA Modules:
  0.0 814.4 jit_solution(17682458878577789062)
XLA Ops:
  7.2 4.4 copy.10
  11.7 4.7 fusion.32
  18.7 25.4 %scatter_custom_fusion = f32[128,192]{0,1:T(8,128)S(1)} fusion(s32[4608]{0:T(1024)S(1)} %fusion.44, f32[4608,128]{1,0:T(8,128)} %bitcast.136, f32[]{:T(128)} %constant.79.clone.1), kind=kCustom, calls=%fused_computation.44 | custom fusion | flops 589824 | bytes 98816 | tf_op jit(solution)/shard_map/scatter-add | solution.py:77
  44.1 4.9 collective-permute-start.2
  54.2 349.1 %while.36 = (s32[]{:T(128)}, bf16[128,64]{0,1:T(8,128)(2,1)S(1)}, bf16[1,128,64]{1,2,0:T(8,128)(2,1)}, bf16[1,128,64]{1,2,0:T(8,128)(2,1)S(1)}, f32[1,64]{1,0:T(...) while((s32[]{:T(128)}, bf16[128,64]{0,1:T(8,128)(2,1)S(1)}, ...), condition=%wide.region_2.3_spmd.clone, body=%wide.region_1.2_spmd.clone.sunk | while | flops 67182600 | bytes 4964833 | solution.py:110
  54.9 83.0 %all-gather.3.cloned.1.call-done = bf16[128,4096]{0,1:T(8,128)(2,1)} async-done(((bf16[128,64]{0,1:T(8,128)(2,1)}), bf16[128,4096]{0,1:T(8,128)(2,1)}) %all-gather.3.cloned.1.call-update) | async-done | bytes 1048592 | tf_op jit(solution)/shard_map/while/body/eval_jaxpr/all_gather | solution.py:32
  140.1 3.1 collective-permute-start
  144.8 79.7 %all-gather.3.cloned.1.call-done = bf16[128,4096]{0,1:T(8,128)(2,1)} async-done(((bf16[128,64]{0,1:T(8,128)(2,1)}), bf16[128,4096]{0,1:T(8,128)(2,1)}) %all-gather.3.cloned.1.call-update) | async-done | bytes 1048592 | tf_op jit(solution)/shard_map/while/body/eval_jaxpr/all_gather | solution.py:32
  231.3 79.7 %all-gather.3.cloned.1.call-done = bf16[128,4096]{0,1:T(8,128)(2,1)} async-done(((bf16[128,64]{0,1:T(8,128)(2,1)}), bf16[128,4096]{0,1:T(8,128)(2,1)}) %all-gather.3.cloned.1.call-update) | async-done | bytes 1048592 | tf_op jit(solution)/shard_map/while/body/eval_jaxpr/all_gather | solution.py:32
  313.1 3.1 collective-permute-start
  317.7 79.4 %all-gather.3.cloned.1.call-done = bf16[128,4096]{0,1:T(8,128)(2,1)} async-done(((bf16[128,64]{0,1:T(8,128)(2,1)}), bf16[128,4096]{0,1:T(8,128)(2,1)}) %all-gather.3.cloned.1.call-update) | async-done | bytes 1048592 | tf_op jit(solution)/shard_map/while/body/eval_jaxpr/all_gather | solution.py:32
  408.8 343.5 %while.37 = (s32[]{:T(128)}, bf16[128,64]{0,1:T(8,128)(2,1)S(1)}, bf16[1,128,64]{1,2,0:T(8,128)(2,1)S(1)}, bf16[1,128,64]{1,2,0:T(8,128)(2,1)S(1)}, f32[1,64]{1,...) while((s32[]{:T(128)}, bf16[128,64]{0,1:T(8,128)(2,1)S(1)}, ...), condition=%wide.region_4.5_spmd.clone, body=%wide.region_3.4_spmd.clone.sunk | while | flops 67239936 | bytes 5046789 | solution.py:136
  409.5 79.3 %all-gather.5.cloned.1.call-done = bf16[128,4096]{0,1:T(8,128)(2,1)} async-done(((bf16[128,64]{0,1:T(8,128)(2,1)}), bf16[128,4096]{0,1:T(8,128)(2,1)}) %all-gather.5.cloned.1.call-update) | async-done | bytes 1048592 | tf_op jit(solution)/shard_map/while/body/eval_jaxpr/all_gather | solution.py:32
  495.5 78.9 %all-gather.5.cloned.1.call-done = bf16[128,4096]{0,1:T(8,128)(2,1)} async-done(((bf16[128,64]{0,1:T(8,128)(2,1)}), bf16[128,4096]{0,1:T(8,128)(2,1)}) %all-gather.5.cloned.1.call-update) | async-done | bytes 1048592 | tf_op jit(solution)/shard_map/while/body/eval_jaxpr/all_gather | solution.py:32
  581.2 79.1 %all-gather.5.cloned.1.call-done = bf16[128,4096]{0,1:T(8,128)(2,1)} async-done(((bf16[128,64]{0,1:T(8,128)(2,1)}), bf16[128,4096]{0,1:T(8,128)(2,1)}) %all-gather.5.cloned.1.call-update) | async-done | bytes 1048592 | tf_op jit(solution)/shard_map/while/body/eval_jaxpr/all_gather | solution.py:32
  667.1 79.1 %all-gather.5.cloned.1.call-done = bf16[128,4096]{0,1:T(8,128)(2,1)} async-done(((bf16[128,64]{0,1:T(8,128)(2,1)}), bf16[128,4096]{0,1:T(8,128)(2,1)}) %all-gather.5.cloned.1.call-update) | async-done | bytes 1048592 | tf_op jit(solution)/shard_map/while/body/eval_jaxpr/all_gather | solution.py:32
  752.3 3.3 collective-permute-start.7
  758.6 10.2 %gather_fusion = bf16[4608,128]{1,0:T(8,128)(2,1)} fusion(bf16[128,192]{0,1:T(8,128)(2,1)S(1)} %maximum_bitcast_fusion, s32[5120]{0:T(1024)S(1)} %pad_clamp_fusion), kind=kCustom, calls=%fused_computation.clone | custom fusion | bytes 2377728 | tf_op jit(solution)/shard_map/jit(_take)/gather | solution.py:43
  768.8 10.2 %gather_fusion.1 = bf16[4608,128]{1,0:T(8,128)(2,1)} fusion(bf16[128,192]{0,1:T(8,128)(2,1)S(1)} %maximum_bitcast_fusion.1, s32[5120]{0:T(1024)S(1)} %pad_clamp_fusion), kind=kCustom, calls=%fused_computation.1.clone | custom fusion | bytes 2377728 | tf_op jit(solution)/shard_map/jit(_take)/gather | solution.py:43
  779.0 4.7 broadcast_select_fusion.1
  783.6 7.2 fusion.7
  790.8 8.2 %fusion.5 = bf16[128,36,256]{2,0,1:T(8,128)(2,1)} fusion(f32[36,128,256]{2,1,0:T(8,128)} %fusion.7, bf16[36,128,256]{2,1,0:T(8,128)(2,1)} %copy-done.2, bf16[1,36,256,256]{3,2,1,0:T(8,128)(2,1)} %param.16, bf16[128,36,128]{0,2,1:T(8,128)(2,1)S(1)} %bitcast.134, bf16[1,36,128,256]{3,2,1,0:T(8,128)(2,1)S(1)} %copy-done), kind=kOutput, calls=%fused_computation.17 | convolution fusion | flops 914227200 | bytes 17694720 | tf_op jit(solution)/shard_map/jab,sjb->sja/dot_general | solution.py:27
  799.0 4.3 copy.12
  803.3 4.3 copy.13
  (96 shorter events, 63.6 us)
Async XLA Ops:
  16.5 37.7 %copy-start.1 = (bf16[1,64,4096]{2,1,0:T(8,128)(2,1)S(1)}, bf16[1,64,4096]{2,1,0:T(8,128)(2,1)}, u32[]{:S(2)}) copy-start(bf16[1,64,4096]{2,1,0:T(8,128)(2,1)} %param.15) | copy-start | bytes 1572868
  16.5 37.7 %copy-start.4 = (bf16[1,128,64]{1,2,0:T(8,128)(2,1)S(1)}, bf16[1,128,64]{1,2,0:T(8,128)(2,1)}, u32[]{:S(2)}) copy-start(bf16[1,128,64]{1,2,0:T(8,128)(2,1)} %param.13) | copy-start | bytes 49156
  44.1 7.6 collective-permute-start.2
  49.0 5.1 collective-permute-start.3
  54.2 83.7 %all-gather.3.cloned.1.call-start = ((), (), s32[]{:S(2)}) async-start(), calls=%async_computation | async-start | bytes 1064960 | tf_op jit(solution)/shard_map/while/body/eval_jaxpr/all_gather | solution.py:32
  140.1 3.9 collective-permute-start
  144.0 80.4 %all-gather.3.cloned.1.call-start = ((), (), s32[]{:S(2)}) async-start(), calls=%async_computation | async-start | bytes 1064960 | tf_op jit(solution)/shard_map/while/body/eval_jaxpr/all_gather | solution.py:32
  226.6 3.9 collective-permute-start
  230.5 80.4 %all-gather.3.cloned.1.call-start = ((), (), s32[]{:S(2)}) async-start(), calls=%async_computation | async-start | bytes 1064960 | tf_op jit(solution)/shard_map/while/body/eval_jaxpr/all_gather | solution.py:32
  313.1 3.9 collective-permute-start
  317.0 80.1 %all-gather.3.cloned.1.call-start = ((), (), s32[]{:S(2)}) async-start(), calls=%async_computation | async-start | bytes 1064960 | tf_op jit(solution)/shard_map/while/body/eval_jaxpr/all_gather | solution.py:32
  399.3 3.9 collective-permute-start
  403.2 354.6 %collective-permute-start.5 = (bf16[1,128,64]{1,2,0:T(8,128)(2,1)}, bf16[1,128,64]{1,2,0:T(8,128)(2,1)S(1)}, u32[]{:S(2)}, u32[]{:S(2)}) collective-permute-start(bf16[1,128,64]{1,2,0:T(8,128)(2,1)} %get-tuple-element.580), channel_id=1, source_target_pairs={{1,0},{2,1},{3,2},{4,3},{5,4},{6,5},{7,6},{8,7},{9,8},{10,9},{11,1... | collective-permute-start | bytes 49160 | tf_op jit(solution)/shard_map/ppermute | solution.py:15
  406.3 351.6 %collective-permute-start.4 = (bf16[1,128,64]{1,2,0:T(8,128)(2,1)}, bf16[1,128,64]{1,2,0:T(8,128)(2,1)S(1)}, u32[]{:S(2)}, u32[]{:S(2)}) collective-permute-start(bf16[1,128,64]{1,2,0:T(8,128)(2,1)} %get-tuple-element.580), channel_id=1, source_target_pairs={{0,1},{1,2},{2,3},{3,4},{4,5},{5,6},{6,7},{7,8},{8,9},{9,10},{10,1... | collective-permute-start | bytes 49160 | tf_op jit(solution)/shard_map/ppermute | solution.py:14
  408.8 80.0 %all-gather.5.cloned.1.call-start = ((), (), s32[]{:S(2)}) async-start(), calls=%async_computation.1 | async-start | bytes 1064960 | tf_op jit(solution)/shard_map/while/body/eval_jaxpr/all_gather | solution.py:32
  490.3 4.5 collective-permute-start.1
  494.8 79.6 %all-gather.5.cloned.1.call-start = ((), (), s32[]{:S(2)}) async-start(), calls=%async_computation.1 | async-start | bytes 1064960 | tf_op jit(solution)/shard_map/while/body/eval_jaxpr/all_gather | solution.py:32
  575.9 4.5 collective-permute-start.1
  580.4 79.9 %all-gather.5.cloned.1.call-start = ((), (), s32[]{:S(2)}) async-start(), calls=%async_computation.1 | async-start | bytes 1064960 | tf_op jit(solution)/shard_map/while/body/eval_jaxpr/all_gather | solution.py:32
  661.9 4.5 collective-permute-start.1
  666.4 79.9 %all-gather.5.cloned.1.call-start = ((), (), s32[]{:S(2)}) async-start(), calls=%async_computation.1 | async-start | bytes 1064960 | tf_op jit(solution)/shard_map/while/body/eval_jaxpr/all_gather | solution.py:32
  747.8 4.5 collective-permute-start.1
  752.3 16.5 %collective-permute-start.7 = (bf16[1,128,64]{1,2,0:T(8,128)(2,1)S(1)}, bf16[1,128,64]{1,2,0:T(8,128)(2,1)S(1)}, u32[]{:S(2)}, u32[]{:S(2)}) collective-permute-start(bf16[1,128,64]{1,2,0:T(8,128)(2,1)S(1)} %get-tuple-element.336), channel_id=1, source_target_pairs={{1,0},{2,1},{3,2},{4,3},{5,4},{6,5},{7,6},{8,7},{9,8},{10,9},{11,1... | collective-permute-start | bytes 49160 | tf_op jit(solution)/shard_map/ppermute | solution.py:15
  755.6 13.2 %collective-permute-start.6 = (bf16[1,128,64]{1,2,0:T(8,128)(2,1)S(1)}, bf16[1,128,64]{1,2,0:T(8,128)(2,1)S(1)}, u32[]{:S(2)}, u32[]{:S(2)}) collective-permute-start(bf16[1,128,64]{1,2,0:T(8,128)(2,1)S(1)} %get-tuple-element.336), channel_id=1, source_target_pairs={{0,1},{1,2},{2,3},{3,4},{4,5},{5,6},{6,7},{7,8},{8,9},{9,10},{10,1... | collective-permute-start | bytes 49160 | tf_op jit(solution)/shard_map/ppermute | solution.py:14
  (10 other events, 82.7 us)
Sparse Core Ops, SparseCore 0:
  58.3 79.5 all-gather.2
  148.2 76.2 all-gather.2
  234.7 76.2 all-gather.2
  320.9 76.2 all-gather.2
  412.7 76.0 all-gather.4
  498.7 75.6 all-gather.4
  584.6 75.6 all-gather.4
  670.5 75.6 all-gather.4
where the time goes:
time: 816 us; the launch traced here: 814 us
  waiting for transfers between devices  654 us (80%)
  other arithmetic  37.2 us (5%)
  matrix products  37.1 us (5%)
  local copies, waits for them, and re-layouts  35.7 us (4%)
  starting transfers between devices  35.5 us (4%)
  between operations  14.3 us (2%)
    all_gather x8, waiting for transfers between devices, top_fold(): lax.all_gather(vectors, 'front', axis=1, tiled=True)  638 us
    scatter-add x1, other arithmetic, body(): window_one.at[:, local_rows[panel_index].reshape(-1)]  25.4 us
    ppermute x10, starting transfers between devices, passed_along(): return lax.ppermute(block, axis, route)  24.3 us
    gather x2, local copies, waits for them, and re-layouts, lift_through(): jnp.take(window[0], flat_rows, axis=1)  20.3 us
    dot_general x3, matrix products, leaf_apply(): jnp.einsum('jab,sjb->sja', inverse_blocks, vectors, preferred_element_typ...  20.1 us
  transfers between devices with their start and end apart: 22, of which 17 were waited for; matrix products, arithmetic and copies ran while one was open for 3% of the time, Pallas kernels for 0%

commit v1 on v0

v1 whole, which is shorter than its diff:
```python
import functools

import jax
import jax.numpy as jnp
from jax import lax
from jax.experimental import pallas as pl
from jax.experimental.pallas import tpu as pltpu
from jax.sharding import PartitionSpec as P

MESH = pl.DeviceIdType.MESH
BF = jnp.bfloat16
F32 = jnp.float32
NT = (((1,), (1,)), ((), ()))
NN = (((1,), (0,)), ((), ()))
STEPS = 7
GROUP = 16


def dot(a, b, dims):
    return lax.dot_general(a, b, dims, preferred_element_type=F32)


def kernel(
    sizes,
    ts_hbm, ls_hbm, ti_hbm, li_hbm, bd_hbm, tr_hbm, cp_hbm,
    tf_hbm, lf_hbm,
    ts, vec, inv, bnd, rows, cpl,
    inner, lift, acc, main, halo, main_in, halo_in, tops, gath, tabs, field, own_w, nb_w, half,
    in_sem, small_sem, out_sem,
    ta_send, ta_recv, tc_send, tc_recv,
    pm_send, pm_recv, ph_send, ph_recv,
    z_send, y_send, g_recv, o_send, o_recv,
):
    ny, nz, chunks, per = sizes
    chips = ny * nz
    panels = 4
    r = lax.axis_index("panel")
    f = lax.axis_index("front")
    m, c = lax.div(f, 2), lax.rem(f, 2)
    y, z = lax.div(m, nz), lax.rem(m, nz)
    other = 1 - c
    up, down = lax.rem(m + 1, chips), lax.rem(m + chips - 1, chips)
    side = lax.rem(m + chips - 1 + 2 * c, chips)

    def dev(q, chip, core):
        return (q, chip * 2 + core)

    def remote(src, dst, send, recv, where):
        return pltpu.make_async_remote_copy(
            src_ref=src, dst_ref=dst, send_sem=send, recv_sem=recv,
            device_id=where, device_id_type=MESH,
        )

    width = ls_hbm.shape[2] // chunks // per

    small = [
        pltpu.make_async_copy(ts_hbm.at[0], ts, small_sem.at[0]),
        pltpu.make_async_copy(tr_hbm.at[0], rows, small_sem.at[1]),
        pltpu.make_async_copy(cp_hbm, cpl, small_sem.at[2]),
        pltpu.make_async_copy(
            ti_hbm.at[0], tops.at[r, pl.ds(pl.multiple_of(c * 64, 64), 64)], small_sem.at[3]
        ),
    ]
    big = []
    for g in range(chunks):
        at = pl.ds(g * per, per)
        cols = pl.ds(g * per * width, per * width)
        big.append((
            pltpu.make_async_copy(bd_hbm.at[0, at], bnd.at[at], in_sem.at[0, g]),
            pltpu.make_async_copy(li_hbm.at[0, at], inv.at[at], in_sem.at[1, g]),
            pltpu.make_async_copy(ls_hbm.at[0, :, cols], vec.at[:, cols], in_sem.at[2, g]),
        ))
    small[1].start()
    for copy in big[0]:
        copy.start()
    for copy in (small[0], small[2], small[3]):
        copy.start()
    for group in big[1:]:
        for copy in group:
            copy.start()

    barrier = pltpu.get_barrier_semaphore()
    count = 0
    for dq in range(panels):
        q = lax.rem(r + dq, panels)
        for core in (c, other):
            for chip in (m, up, down):
                if dq == 0 and core is c and chip is m:
                    continue
                pl.semaphore_signal(barrier, inc=1, device_id=dev(q, chip, core), device_id_type=MESH)
                count += 1
    for dz in range(1, nz):
        peer = dev(r, y * nz + lax.rem(z + dz, nz), c)
        pl.semaphore_signal(barrier, inc=1, device_id=peer, device_id_type=MESH)
        count += 1
    for dy in range(1, ny):
        peer = dev(r, lax.rem(y + dy, ny) * nz + z, c)
        pl.semaphore_signal(barrier, inc=1, device_id=peer, device_id_type=MESH)
        count += 1
    pl.semaphore_wait(barrier, count)

    right, left, far = lax.rem(r + 1, 4), lax.rem(r + 3, 4), lax.rem(r + 2, 4)

    def rows_of(q, core, start=0, size=64):
        return tops.at[q, pl.ds(pl.multiple_of(core * 64 + start, 32), size)]

    sent_a = [
        remote(ti_hbm.at[0], rows_of(r, c), ta_send.at[0], ta_recv.at[0], dev(right, m, c)),
        remote(ti_hbm.at[0], rows_of(r, c), ta_send.at[1], ta_recv.at[1], dev(left, m, c)),
        remote(ti_hbm.at[0], rows_of(r, c), tc_send.at[0], tc_recv.at[0], dev(r, m, other)),
    ]
    for copy in sent_a:
        copy.start()

    acc[...] = jnp.zeros_like(acc)
    base = m * 128
    small[1].wait()

    def leaf(j):
        u = jnp.bitwise_and(rows[pl.ds(j, 1), :] - base, 255)
        hot = lax.broadcasted_iota(jnp.int32, (256, u.shape[1]), 0) == u
        hot = jnp.where(hot, 1.0, 0.0).astype(BF)
        spread = dot(hot, bnd[j], NN).astype(BF)
        cols = pl.ds(pl.multiple_of(j * width, width), width)
        both = dot(jnp.concatenate([vec[:, cols], spread], axis=0), inv[j], NT).astype(BF)
        inner[:, cols] = both[:128]
        lift[:, cols] = both[128:]
        return dot(both[:128], spread, NT)

    for g in range(chunks):
        for copy in big[g]:
            copy.wait()

        def body(i, carry):
            first = g * per + i * 3
            acc[...] += leaf(first) + leaf(first + 1) + leaf(first + 2)
            return carry

        lax.fori_loop(0, per // 3, body, 0)

    for k in (0, 2):
        small[k].wait()
    known = -acc[:, :128]
    local = ts[...].astype(F32)
    zero = jnp.zeros_like(local)
    lower = jnp.where(c == 0, local, zero)
    upper = jnp.where(c == 0, zero, local)
    known = known + jnp.concatenate([lower, upper], axis=1)
    scale = cpl[...]
    blank = jnp.zeros_like(scale)
    scale = jnp.concatenate(
        [jnp.where(c == 0, scale, blank), jnp.where(c == 0, blank, scale)], axis=1
    )
    scale = jnp.broadcast_to(scale, (8, 128))
    for k in range(8):
        main[k, :GROUP] = known[k * GROUP : (k + 1) * GROUP]
        main[k, GROUP:] = scale
        halo[k] = -acc[k * GROUP : (k + 1) * GROUP, 128:]
    mine = r * 2 + c
    main_in[r, c] = main[mine]

    piece_sends = []
    for dq in range(panels):
        q = lax.rem(r + dq, panels)
        for n, core in enumerate((c, other)):
            k, slot = q * 2 + core, dq * 2 + n
            if slot:
                piece_sends.append(remote(
                    main.at[k], main_in.at[r, c], pm_send.at[slot], pm_recv.at[r, c], dev(q, m, core)
                ))
            piece_sends.append(remote(
                halo.at[k], halo_in.at[r, c], ph_send.at[slot], ph_recv.at[r, c], dev(q, side, core)
            ))
    for copy in piece_sends:
        copy.start()

    sent_a[0].wait_recv()
    relays = [
        remote(rows_of(left, c, 0, 32), rows_of(left, c, 0, 32), ta_send.at[2], ta_recv.at[2], dev(right, m, c)),
        remote(rows_of(left, c), rows_of(left, c), tc_send.at[1], tc_recv.at[1], dev(r, m, other)),
    ]
    for copy in relays:
        copy.start()
    sent_a[1].wait_recv()
    more = [
        remote(rows_of(right, c, 32, 32), rows_of(right, c, 32, 32), ta_send.at[3], ta_recv.at[3], dev(left, m, c)),
        remote(rows_of(right, c), rows_of(right, c), tc_send.at[2], tc_recv.at[2], dev(r, m, other)),
    ]
    for copy in more:
        copy.start()
    relays += more

    def finish_tops():
        small[3].wait()
        last = remote(rows_of(far, c), rows_of(far, c), tc_send.at[3], tc_recv.at[3], dev(r, m, other))
        relays[0].wait_recv()
        relays[2].wait_recv()
        last.start()
        for copy in (sent_a[2], relays[1], relays[3], last):
            copy.wait_recv()
        for copy in sent_a + relays + [last]:
            copy.wait_send()

    def meet_pieces(p):
        for core in (0, 1):
            arrival = remote(main.at[0], main_in.at[p, core], pm_send.at[0], pm_recv.at[p, core], dev(r, m, other))

            @pl.when(jnp.logical_or(p != r, c != core))
            def _():
                arrival.wait_recv()

            remote(halo.at[0], halo_in.at[p, core], ph_send.at[0], ph_recv.at[p, core], dev(r, m, other)).wait_recv()
        a, b = main_in[p, 0], main_in[p, 1]
        tabs[p] = a[:GROUP] + b[:GROUP] + halo_in[p, 0] + halo_in[p, 1]
        pair = a[GROUP:] + b[GROUP:]
        tabs[4 + p] = jnp.concatenate([pair, pair], axis=0)

    def z_copy(t, s, dz):
        return remote(
            gath.at[t, m], gath.at[t, m], z_send.at[s, dz - 1], g_recv.at[s, m],
            dev(r, y * nz + lax.rem(z + dz, nz), c),
        )

    def y_copy(t, s, dz, dy):
        tile = y * nz + lax.rem(z + dz, nz)
        return remote(
            gath.at[t, tile], gath.at[t, tile], y_send.at[s, dz, dy - 1], g_recv.at[s, tile],
            dev(r, lax.rem(y + dy, ny) * nz + z, c),
        )

    near = sorted(range(1, nz), key=lambda d: min(d, nz - d))

    def wait_sends(t, s):
        for dz in range(nz):
            if dz:
                z_copy(t, s, dz).wait_send()
            for dy in range(1, ny):
                y_copy(t, s, dz, dy).wait_send()

    def arrived(t, s, tile):
        remote(gath.at[t, tile], gath.at[t, tile], z_send.at[s, 0], g_recv.at[s, tile], dev(r, m, other)).wait_recv()

    def block(t, p, row):
        x = jnp.concatenate([gath[t, row * nz + i] for i in range(nz)], axis=1)
        cols = pl.ds(pl.multiple_of(row * (nz * 128), nz * 128), nz * 128)
        return dot(x, tops[p, :, cols], NT)

    def solve(t, p, value, extra):
        s = lax.rem(t, 2)
        gath[t, m] = value
        for dz in reversed(near):
            z_copy(t, s, dz).start()
        for dy in range(1, ny):
            y_copy(t, s, 0, dy).start()
        extra()
        for dz in near:
            arrived(t, s, y * nz + lax.rem(z + dz, nz))
            for dy in range(1, ny):
                y_copy(t, s, dz, dy).start()
        total = block(t, p, y)
        for dy in range(1, ny):
            row = lax.rem(y + dy, ny)
            for i in range(nz):
                arrived(t, s, row * nz + lax.rem(z + i, nz))
            total += block(t, p, row)
        return total

    def send_field(p, value):
        field[p] = value.astype(BF)
        mine = r * 2 + c

        @pl.when(p == r)
        def _():
            own_w[mine] = value.astype(BF)

        @pl.when(p != r)
        def _():
            remote(field.at[p], own_w.at[mine], o_send.at[p, 0], o_recv.at[mine, 0], dev(p, m, c)).start()

        for copy in field_copies(p):
            copy.start()

    def field_copies(p):
        mine = r * 2 + c
        return [
            remote(field.at[p], own_w.at[mine], o_send.at[p, 1], o_recv.at[mine, 0], dev(p, m, other)),
            remote(field.at[p], nb_w.at[mine], o_send.at[p, 2], o_recv.at[mine, 1], dev(p, down, 1)),
            remote(field.at[p], nb_w.at[mine], o_send.at[p, 3], o_recv.at[mine, 1], dev(p, up, 0)),
        ]

    tabs[12] = jnp.zeros((GROUP, 128), F32)

    def forward(t, carry):
        meet_pieces(t)
        value = (tabs[t] + tabs[4 + t] * tabs[12]).astype(BF)

        def extra():
            @pl.when(t == 0)
            def _():
                for k, copy in enumerate(piece_sends):
                    copy.wait_send()

            @pl.when(t > 0)
            def _():
                wait_sends(t - 1, lax.rem(t + 1, 2))

        def first():
            @pl.when(t == 0)
            def _():
                finish_tops()

        top = solve_with(t, t, value, extra, first).astype(BF).astype(F32)
        tabs[8 + t] = top
        tabs[12] = top
        return carry

    def solve_with(t, p, value, extra, first):
        def both():
            extra()
            first()

        return solve(t, p, value, both)

    lax.fori_loop(0, panels, forward, 0)

    nothing = jnp.zeros((GROUP, chips * 128), BF)
    fix = dot(nothing, tops[3], NT).astype(BF).astype(F32)
    top = (tabs[12] + fix).astype(BF).astype(F32)
    tabs[12] = top
    send_field(jnp.int32(3), top)

    def backward(t, carry):
        p = 6 - t
        value = (tabs[5 + p] * tabs[12]).astype(BF)
        fixed = solve(t, p, value, lambda: wait_sends(t - 1, lax.rem(t + 1, 2))).astype(BF).astype(F32)
        top = (tabs[8 + p] + fixed).astype(BF).astype(F32)
        tabs[12] = top
        send_field(p, top)
        return carry

    lax.fori_loop(4, STEPS, backward, 0)
    wait_sends(STEPS - 1, (STEPS - 1) % 2)

    for k in range(8):
        @pl.when(k != r * 2 + c)
        def _():
            remote(field.at[0], own_w.at[k], o_send.at[0, 0], o_recv.at[k, 0], dev(r, m, other)).wait_recv()

        remote(field.at[0], nb_w.at[k], o_send.at[0, 0], o_recv.at[k, 1], dev(r, m, other)).wait_recv()
    for p in range(panels):
        @pl.when(p != r)
        def _():
            remote(field.at[p], own_w.at[0], o_send.at[p, 0], o_recv.at[0, 0], dev(r, m, other)).wait_send()

        for copy in field_copies(p):
            copy.wait_send()

    own = own_w[...].reshape(128, 128)
    window = jnp.concatenate([own, nb_w[...].reshape(128, 128)], axis=1)
    half[...] = jnp.where(c == 0, own[:, :64], own[:, 64:])
    top_out = pltpu.make_async_copy(half, tf_hbm.at[0], out_sem.at[chunks])
    top_out.start()
    outs = []
    for g in range(chunks):
        cols = slice(g * per * width, (g + 1) * per * width)
        vec[:, cols] = (inner[:, cols].astype(F32) - dot(window, lift[:, cols], NN)).astype(BF)
        outs.append(pltpu.make_async_copy(vec.at[:, cols], lf_hbm.at[0, :, cols], out_sem.at[g]))
        outs[-1].start()
    for copy in outs:
        copy.wait()
    top_out.wait()


def body(sizes, top_source, leaf_source, top_inverse, leaf_inverse, boundary, touch_rows, coupling):
    ny, nz, chunks, per = sizes
    leaves, width = leaf_inverse.shape[1:3]
    reach = boundary.shape[2]
    columns = leaves * width
    order = ny * nz * 128
    any_spec = pl.BlockSpec(memory_space=pl.ANY)
    dma = pltpu.SemaphoreType.DMA
    vmem = pltpu.VMEM
    return pl.pallas_call(
        functools.partial(kernel, sizes),
        out_shape=(
            jax.ShapeDtypeStruct(top_source.shape, BF),
            jax.ShapeDtypeStruct(leaf_source.shape, BF),
        ),
        in_specs=[any_spec] * 7,
        out_specs=(any_spec, any_spec),
        scratch_shapes=[
            vmem((128, 64), BF),
            vmem((128, columns), BF),
            vmem((leaves, width, width), BF),
            vmem((leaves, reach, width), BF),
            vmem((leaves, reach), jnp.int32),
            vmem((1, 64), F32),
            vmem((128, columns), BF),
            vmem((256, columns), BF),
            vmem((128, 256), F32),
            vmem((8, GROUP + 8, 128), F32),
            vmem((8, GROUP, 128), F32),
            vmem((4, 2, GROUP + 8, 128), F32),
            vmem((4, 2, GROUP, 128), F32),
            vmem((4, 128, order), BF),
            vmem((STEPS, ny * nz, GROUP, 128), BF),
            vmem((16, GROUP, 128), F32),
            vmem((4, GROUP, 128), BF),
            vmem((8, GROUP, 128), BF),
            vmem((8, GROUP, 128), BF),
            vmem((128, 64), BF),
            dma((3, chunks)), dma((4,)), dma((chunks + 1,)),
            dma((4,)), dma((4,)), dma((4,)), dma((4,)),
            dma((8,)), dma((4, 2)), dma((8,)), dma((4, 2)),
            dma((2, nz - 1)), dma((2, nz, ny - 1)), dma((2, ny * nz)),
            dma((4, 4)), dma((8, 2)),
        ],
        compiler_params=pltpu.CompilerParams(
            collective_id=0, has_side_effects=True, vmem_limit_bytes=50 * 1024 * 1024
        ),
    )(top_source, leaf_source, top_inverse, leaf_inverse, boundary, touch_rows, coupling)


def solution(mesh, sizes=(4, 8, 6, 6)):
    placed = (
        P("panel", None, "front"),
        P("panel", None, "front"),
        P("panel", "front", None),
        P("panel", "front", None, None),
        P("panel", "front", None, None),
        P("panel", "front", None),
        P("panel", "front"),
    )
    return jax.shard_map(
        functools.partial(body, sizes),
        mesh=mesh,
        in_specs=placed,
        out_specs=(P("panel", None, "front"), P("panel", None, "front")),
        check_vma=False,
    )
```

time: 816 us -> 105 us (0.13)
  waiting for transfers between devices: 654 us -> 0 us
  Pallas kernels: 0 us -> 98.7 us
  other arithmetic: 37.2 us -> 0 us
  matrix products: 37.1 us -> 0 us
  starting transfers between devices: 35.5 us -> 0 us
  local copies, waits for them, and re-layouts: 35.7 us -> 5.35 us
  between operations: 14.3 us -> 0.65 us
    all_gather x8 -> x0, waiting for transfers between devices: 638 us -> none  [top_fold(): lax.all_gather(vectors, 'front', axis=1, tiled=True)]
    pallas_call x0 -> x1, Pallas kernels: none -> 98.7 us  [body(): pl.pallas_call(functools.partial(kernel, sizes), out_shape=(jax.ShapeDtyp...]
    dot_general x12 -> x0, matrix products: 37.1 us -> none  [the longest x3 20.1 us: leaf_apply(): jnp.einsum('jab,sjb->sja', inverse_blocks, vectors, preferred_element_typ...]
    ppermute x14 -> x0, starting transfers between devices: 35.4 us -> none  [the longest x10 24.3 us: passed_along(): return lax.ppermute(block, axis, route)]
    scatter-add x1 -> x0, other arithmetic: 25.4 us -> none  [body(): window_one.at[:, local_rows[panel_index].reshape(-1)]]
    gather x2 -> x0, local copies, waits for them, and re-layouts: 20.3 us -> none  [lift_through(): jnp.take(window[0], flat_rows, axis=1)]
    ppermute x14 -> x0, waiting for transfers between devices: 15.6 us -> none  [the longest x10 15.6 us: passed_along(): return lax.ppermute(block, axis, route)]
  transfers between devices with their start and end apart: 22 -> 0, of which waited for: 17 -> 0; matrix products, arithmetic and copies ran while one was open for 3% -> 0% of each run, Pallas kernels for 0% -> 0%
where the time goes in v1:
time: 105 us
  Pallas kernels  98.7 us (94%)
  local copies, waits for them, and re-layouts  5.35 us (5%)
    pallas_call x1, Pallas kernels, body(): pl.pallas_call(functools.partial(kernel, sizes), out_shape=(jax.ShapeDtyp...  98.7 us
    unnamed x7, local copies, waits for them, and re-layouts  4.65 us

profile of v1, /device:TPU:1, one launch (start us, length us, event | category | flops | bytes accessed | tf_op | source)
XLA Modules:
  0.0 104.7 jit_solution(949224448722567670)
XLA Ops:
  0.6 0.7 copy.10.tr_hbm
  1.4 0.8 copy.9.ts_hbm
  2.2 0.0 copy-start
  2.2 1.0 copy-done
  3.2 0.0 copy-start.1
  3.2 0.7 copy-done.1
  3.9 98.7 %shard_map.86 = (bf16[1,128,64]{2,1,0:T(8,128)(2,1)S(1)}, bf16[1,128,9216]{2,1,0:T(8,128)(2,1)S(1)}) custom-call(bf16[1,128,64]{2,1,0:T(8,128)(2,1)S(1)} %copy.9.ts_hbm, bf16[1,128,9216]{2,1,0:T(8,128)(2,1)} %ls_hbm.1, bf16[1,64,4096]{2,1,0:T(8,128)(2,1)S(1)} %copy-done, bf16[1,36,256,256]{3,2,1,0:T(8,128)(2,1)} %li_hbm.1, bf16[1,36,128,256]{3,2,1,0:T(8,128)(2,1)} %bd_hbm.1, ...), custom_call_target="tpu_custom_call" | custom-call | tf_op jit(solution)/shard_map/pallas_call | solution.py:383
  102.6 0.7 copy.11
  103.3 1.4 %copy.13 = bf16[1,128,9216]{2,1,0:T(8,128)(2,1)} copy(bf16[1,128,9216]{2,1,0:T(8,128)(2,1)S(1)} %get-tuple-element.7) | data formatting | bytes 4718592
Async XLA Ops:
  2.2 1.1 %copy-start = (bf16[1,64,4096]{2,1,0:T(8,128)(2,1)S(1)}, bf16[1,64,4096]{2,1,0:T(8,128)(2,1)}, u32[]{:S(2)}) copy-start(bf16[1,64,4096]{2,1,0:T(8,128)(2,1)} %ti_hbm.1) | copy-start | bytes 1572868
  3.2 0.7 copy-start.1

commit v2 on v1

v2 whole, which is shorter than its diff:
```python
import functools

import jax
import jax.numpy as jnp
from jax import lax
from jax.experimental import pallas as pl
from jax.experimental.pallas import tpu as pltpu
from jax.sharding import PartitionSpec as P

MESH = pl.DeviceIdType.MESH
BF = jnp.bfloat16
F32 = jnp.float32
NT = (((1,), (1,)), ((), ()))
NN = (((1,), (0,)), ((), ()))
STEPS = 7
GROUP = 16


def dot(a, b, dims):
    return lax.dot_general(a, b, dims, preferred_element_type=F32)


def kernel(
    sizes,
    ts_hbm, ls_hbm, ti_hbm, li_hbm, bd_hbm, tr_hbm, cp_hbm,
    tf_hbm, lf_hbm,
    ts, vec, inv, bnd, rows, cpl,
    inner, lift, acc, main, halo, main_in, halo_in, tops, gath, tabs, field, own_w, nb_w, half,
    in_sem, small_sem, out_sem,
    ta_send, ta_recv, tc_send, tc_recv,
    pm_send, pm_recv, ph_send, ph_recv,
    g_send, g_recv, o_send, o_recv,
):
    ny, nz, chunks, per = sizes
    chips = ny * nz
    panels = 4
    r = lax.axis_index("panel")
    f = lax.axis_index("front")
    m, c = lax.div(f, 2), lax.rem(f, 2)
    y, z = lax.div(m, nz), lax.rem(m, nz)
    other = 1 - c
    up, down = lax.rem(m + 1, chips), lax.rem(m + chips - 1, chips)
    side = lax.rem(m + chips - 1 + 2 * c, chips)

    def dev(q, chip, core):
        return (q, chip * 2 + core)

    def chip_at(dy, dz):
        return lax.rem(y + dy, ny) * nz + lax.rem(z + dz, nz)

    steps_away = sorted(
        ((dy, dz) for dy in range(ny) for dz in range(nz) if dy or dz),
        key=lambda d: -min(d[0], ny - d[0]) - min(d[1], nz - d[1]),
    )

    def remote(src, dst, send, recv, where):
        return pltpu.make_async_remote_copy(
            src_ref=src, dst_ref=dst, send_sem=send, recv_sem=recv,
            device_id=where, device_id_type=MESH,
        )

    width = ls_hbm.shape[2] // chunks // per

    small = [
        pltpu.make_async_copy(ts_hbm.at[0], ts, small_sem.at[0]),
        pltpu.make_async_copy(tr_hbm, rows, small_sem.at[1]),
        pltpu.make_async_copy(cp_hbm, cpl, small_sem.at[2]),
        pltpu.make_async_copy(
            ti_hbm.at[0], tops.at[r, pl.ds(pl.multiple_of(c * 64, 64), 64)], small_sem.at[3]
        ),
    ]

    def big(g):
        at = pl.ds(g * per, per)
        cols = pl.ds(pl.multiple_of(g * (per * width), per * width), per * width)
        return (
            pltpu.make_async_copy(ls_hbm.at[0, :, cols], vec.at[:, cols], in_sem.at[2, g]),
            pltpu.make_async_copy(li_hbm.at[0, at], inv.at[at], in_sem.at[1, g]),
            pltpu.make_async_copy(bd_hbm.at[0, at], bnd.at[at], in_sem.at[0, g]),
        )

    small[1].start()
    for copy in big(0):
        copy.start()
    for copy in (small[0], small[2], small[3]):
        copy.start()
    for g in range(1, chunks):
        for copy in big(g):
            copy.start()

    barrier = pltpu.get_barrier_semaphore()
    peers = [dev(r, chip_at(dy, dz), c) for dy, dz in steps_away]
    beyond = lax.rem(m + chips + 1 - 2 * c, chips)
    for dq in range(panels):
        q = lax.rem(r + dq, panels)
        if dq:
            peers += [dev(q, m, c), dev(q, side, c), dev(q, beyond, c)]
        peers += [dev(q, m, other), dev(q, side, other)]
    for peer in peers:
        pl.semaphore_signal(barrier, inc=1, device_id=peer, device_id_type=MESH)

    acc[...] = jnp.zeros_like(acc)
    base = m * 128
    small[1].wait()

    def columns_of(j):
        return pl.ds(pl.multiple_of(j * width, width), width)

    def hot_rows(j):
        u = jnp.bitwise_and(rows[j] - base, 255)
        hot = lax.broadcasted_iota(jnp.int32, (256, u.shape[1]), 0) == u
        return jnp.where(hot, 1.0, 0.0).astype(BF)

    def leaf(j):
        solved = dot(vec[:, columns_of(j)], inv[j], NT).astype(BF)
        inner[:, columns_of(j)] = solved
        return dot(solved, bnd[j], NT).astype(BF)

    def leaves(g, carry):
        for copy in big(g):
            copy.wait()
        first = g * per
        pushed = jnp.concatenate([leaf(first + i) for i in range(per)], axis=1)
        hot = jnp.concatenate([hot_rows(first + i) for i in range(per)], axis=1)
        acc[...] += dot(pushed, hot, NT)
        return carry

    def lifts(g):
        for i in range(per):
            j = g * per + i
            spread = dot(hot_rows(j), bnd[j], NN).astype(BF)
            lift[:, columns_of(j)] = dot(spread, inv[j], NT).astype(BF)

    early = chunks // 3
    lax.fori_loop(0, early, leaves, 0)
    pl.semaphore_wait(barrier, len(peers))

    right, left, far = lax.rem(r + 1, 4), lax.rem(r + 3, 4), lax.rem(r + 2, 4)

    def rows_of(q, core, start=0, size=32):
        return tops.at[q, pl.ds(pl.multiple_of(core * 64 + start, 32), size)]

    def across(n, q, start, to, fresh):
        dst = rows_of(q, c, start)
        src = ti_hbm.at[0, pl.ds(start, 32)] if fresh else dst
        return remote(src, dst, ta_send.at[n], ta_recv.at[n], dev(to, m, c))

    def share(n, q, start, size=32):
        part = rows_of(q, c, start, size)
        src = ti_hbm.at[0] if size == 64 else part
        return remote(src, part, tc_send.at[n], tc_recv.at[n], dev(r, m, other))

    first_right, first_left = across(0, r, 0, right, True), across(1, r, 32, left, True)
    second_right, second_left = across(2, r, 32, right, True), across(3, r, 0, left, True)
    on_right, on_left = across(4, left, 0, right, False), across(5, right, 32, left, False)
    shares = [
        share(0, r, 0, 64), share(1, left, 0), share(2, right, 32), share(3, left, 32),
        share(4, right, 0), share(5, far, 0), share(6, far, 32),
    ]
    first_right.start()
    first_left.start()
    shares[0].start()

    lax.fori_loop(early, chunks, leaves, 0)

    for k in (0, 2):
        small[k].wait()
    known = -acc[:, :128]
    local = ts[...].astype(F32)
    zero = jnp.zeros_like(local)
    lower = jnp.where(c == 0, local, zero)
    upper = jnp.where(c == 0, zero, local)
    known = known + jnp.transpose(jnp.concatenate([lower, upper], axis=0))
    scale = cpl[...]
    blank = jnp.zeros_like(scale)
    scale = jnp.concatenate(
        [jnp.where(c == 0, scale, blank), jnp.where(c == 0, blank, scale)], axis=1
    )
    scale = jnp.broadcast_to(scale, (8, 128))
    for k in range(8):
        main[k, :GROUP] = known[k * GROUP : (k + 1) * GROUP]
        main[k, GROUP:] = scale
        halo[k] = -acc[k * GROUP : (k + 1) * GROUP, 128:]
    mine = r * 2 + c
    main_in[r, c] = main[mine]

    piece_sends = []
    for dq in range(panels):
        q = lax.rem(r + dq, panels)
        for n, core in enumerate((c, other)):
            k, slot = q * 2 + core, dq * 2 + n
            if slot:
                piece_sends.append(remote(
                    main.at[k], main_in.at[r, c], pm_send.at[slot], pm_recv.at[r, c], dev(q, m, core)
                ))
            piece_sends.append(remote(
                halo.at[k], halo_in.at[r, c], ph_send.at[slot], ph_recv.at[r, c], dev(q, side, core)
            ))
    for copy in piece_sends:
        copy.start()

    @pl.when(r == 0)
    def _():
        second_right.start()

    @pl.when(r < 3)
    def _():
        second_left.start()

    first_right.wait_recv()
    on_right.start()
    shares[1].start()
    first_left.wait_recv()
    on_left.start()
    shares[2].start()

    @pl.when(r > 0)
    def _():
        second_right.start()

    @pl.when(r == 3)
    def _():
        second_left.start()

    def meet_tops(t):
        away = lax.rem(t + panels - r, panels)

        @pl.when(away == 0)
        def _():
            small[3].wait()
            shares[0].wait_recv()

        @pl.when(away == 1)
        def _():
            second_left.wait_recv()
            shares[4].start()
            shares[2].wait_recv()
            shares[4].wait_recv()

        @pl.when(away == 2)
        def _():
            on_right.wait_recv()
            shares[5].start()
            on_left.wait_recv()
            shares[6].start()
            shares[5].wait_recv()
            shares[6].wait_recv()

        @pl.when(away == 3)
        def _():
            second_right.wait_recv()
            shares[3].start()
            shares[1].wait_recv()
            shares[3].wait_recv()

    def meet_pieces(p):
        for core in (0, 1):
            arrival = remote(main.at[0], main_in.at[p, core], pm_send.at[0], pm_recv.at[p, core], dev(r, m, other))

            @pl.when(jnp.logical_or(p != r, c != core))
            def _():
                arrival.wait_recv()

            remote(halo.at[0], halo_in.at[p, core], ph_send.at[0], ph_recv.at[p, core], dev(r, m, other)).wait_recv()
        a, b = main_in[p, 0], main_in[p, 1]
        tabs[p] = a[:GROUP] + b[:GROUP] + halo_in[p, 0] + halo_in[p, 1]
        pair = a[GROUP:] + b[GROUP:]
        tabs[4 + p] = jnp.concatenate([pair, pair], axis=0)

    def sends(t, s):
        return [
            remote(gath.at[t, m], gath.at[t, m], g_send.at[s, n], g_recv.at[s, m], dev(r, chip_at(dy, dz), c))
            for n, (dy, dz) in enumerate(steps_away)
        ]

    def wait_sends(t, s):
        for copy in sends(t, s):
            copy.wait_send()

    def arrived(t, s, tile):
        remote(gath.at[t, tile], gath.at[t, tile], g_send.at[s, 0], g_recv.at[s, tile], dev(r, m, other)).wait_recv()

    def solve(t, p, value, meanwhile):
        s = lax.rem(t, 2)
        gath[t, m] = value
        for copy in sends(t, s):
            copy.start()
        meanwhile()
        total = jnp.zeros((GROUP, 128), F32)
        for dy in sorted(range(ny), key=lambda d: min(d, ny - d)):
            row = lax.rem(y + dy, ny)
            for dz in range(nz):
                if dy or dz:
                    arrived(t, s, row * nz + lax.rem(z + dz, nz))
            x = jnp.concatenate([gath[t, row * nz + i] for i in range(nz)], axis=1)
            cols = pl.ds(pl.multiple_of(row * (nz * 128), nz * 128), nz * 128)
            total += dot(x, tops[p, :, cols], NT)
        return total

    def send_field(p, value):
        field[p] = value.astype(BF)
        mine = r * 2 + c

        @pl.when(p == r)
        def _():
            own_w[mine] = value.astype(BF)

        @pl.when(p != r)
        def _():
            remote(field.at[p], own_w.at[mine], o_send.at[p, 0], o_recv.at[mine, 0], dev(p, m, c)).start()

        for copy in field_copies(p):
            copy.start()

    def field_copies(p):
        mine = r * 2 + c
        return [
            remote(field.at[p], own_w.at[mine], o_send.at[p, 1], o_recv.at[mine, 0], dev(p, m, other)),
            remote(field.at[p], nb_w.at[mine], o_send.at[p, 2], o_recv.at[mine, 1], dev(p, down, 1)),
            remote(field.at[p], nb_w.at[mine], o_send.at[p, 3], o_recv.at[mine, 1], dev(p, up, 0)),
        ]

    tabs[12] = jnp.zeros((GROUP, 128), F32)

    def forward(t, carry):
        meet_pieces(t)
        value = (tabs[t] + tabs[4 + t] * tabs[12]).astype(BF)

        def meanwhile():
            @pl.when(t > 0)
            def _():
                wait_sends(t - 1, lax.rem(t + 1, 2))

            lifts(t)
            meet_tops(t)

        top = solve(t, t, value, meanwhile).astype(BF).astype(F32)
        tabs[8 + t] = top
        tabs[12] = top
        return carry

    lax.fori_loop(0, panels, forward, 0)

    nothing = jnp.zeros((GROUP, chips * 128), BF)
    fix = dot(nothing, tops[3], NT).astype(BF).astype(F32)
    top = (tabs[12] + fix).astype(BF).astype(F32)
    tabs[12] = top
    send_field(jnp.int32(3), top)

    def backward(t, carry):
        p = 6 - t
        value = (tabs[5 + p] * tabs[12]).astype(BF)

        def meanwhile():
            wait_sends(t - 1, lax.rem(t + 1, 2))

            @pl.when(t < chunks)
            def _():
                lifts(t)

        fixed = solve(t, p, value, meanwhile).astype(BF).astype(F32)
        top = (tabs[8 + p] + fixed).astype(BF).astype(F32)
        tabs[12] = top
        send_field(p, top)
        return carry

    lax.fori_loop(4, STEPS, backward, 0)
    wait_sends(STEPS - 1, (STEPS - 1) % 2)
    crossed = [first_right, first_left, second_right, second_left, on_right, on_left]
    for copy in piece_sends + crossed + shares:
        copy.wait_send()

    for k in range(8):
        @pl.when(k != r * 2 + c)
        def _():
            remote(field.at[0], own_w.at[k], o_send.at[0, 0], o_recv.at[k, 0], dev(r, m, other)).wait_recv()

        remote(field.at[0], nb_w.at[k], o_send.at[0, 0], o_recv.at[k, 1], dev(r, m, other)).wait_recv()
    for p in range(panels):
        @pl.when(p != r)
        def _():
            remote(field.at[p], own_w.at[0], o_send.at[p, 0], o_recv.at[0, 0], dev(r, m, other)).wait_send()

        for copy in field_copies(p):
            copy.wait_send()

    own = own_w[...].reshape(128, 128)
    window = jnp.concatenate([own, nb_w[...].reshape(128, 128)], axis=1)
    turned = jnp.transpose(own.astype(F32))
    half[...] = jnp.where(c == 0, turned[:64], turned[64:]).astype(BF)
    top_out = pltpu.make_async_copy(half, tf_hbm.at[0], out_sem.at[chunks])
    top_out.start()
    outs = []
    for g in range(chunks):
        cols = slice(g * per * width, (g + 1) * per * width)
        vec[:, cols] = (inner[:, cols].astype(F32) - dot(window, lift[:, cols], NN)).astype(BF)
        outs.append(pltpu.make_async_copy(vec.at[:, cols], lf_hbm.at[0, :, cols], out_sem.at[g]))
        outs[-1].start()
    for copy in outs:
        copy.wait()
    top_out.wait()


def body(sizes, top_source, leaf_source, top_inverse, leaf_inverse, boundary, touch_rows, coupling):
    ny, nz, chunks, per = sizes
    leaves, width = leaf_inverse.shape[1:3]
    reach = boundary.shape[2]
    columns = leaves * width
    order = ny * nz * 128
    any_spec = pl.BlockSpec(memory_space=pl.ANY)
    hbm_spec = pl.BlockSpec(memory_space=pltpu.HBM)
    dma = pltpu.SemaphoreType.DMA
    vmem = pltpu.VMEM
    top, leaf = pl.pallas_call(
        functools.partial(kernel, sizes),
        out_shape=(
            jax.ShapeDtypeStruct((1, 64, 128), BF),
            jax.ShapeDtypeStruct(leaf_source.shape, BF),
        ),
        in_specs=[hbm_spec] * 7,
        out_specs=(any_spec, any_spec),
        scratch_shapes=[
            vmem((64, 128), BF),
            vmem((128, columns), BF),
            vmem((leaves, width, width), BF),
            vmem((leaves, reach, width), BF),
            vmem((leaves, 1, reach), jnp.int32),
            vmem((1, 64), F32),
            vmem((128, columns), BF),
            vmem((256, columns), BF),
            vmem((128, 256), F32),
            vmem((8, GROUP + 8, 128), F32),
            vmem((8, GROUP, 128), F32),
            vmem((4, 2, GROUP + 8, 128), F32),
            vmem((4, 2, GROUP, 128), F32),
            vmem((4, 128, order), BF),
            vmem((STEPS, ny * nz, GROUP, 128), BF),
            vmem((16, GROUP, 128), F32),
            vmem((4, GROUP, 128), BF),
            vmem((8, GROUP, 128), BF),
            vmem((8, GROUP, 128), BF),
            vmem((64, 128), BF),
            dma((3, chunks)), dma((4,)), dma((chunks + 1,)),
            dma((6,)), dma((6,)), dma((7,)), dma((7,)),
            dma((8,)), dma((4, 2)), dma((8,)), dma((4, 2)),
            dma((2, ny * nz - 1)), dma((2, ny * nz)),
            dma((4, 4)), dma((8, 2)),
        ],
        compiler_params=pltpu.CompilerParams(
            collective_id=0, has_side_effects=True, vmem_limit_bytes=50 * 1024 * 1024
        ),
    )(
        jnp.swapaxes(top_source, 1, 2), leaf_source, top_inverse, leaf_inverse, boundary,
        jnp.swapaxes(touch_rows, 0, 1), coupling,
    )
    return jnp.swapaxes(top, 1, 2), leaf


def solution(mesh, sizes=(4, 8, 6, 6)):
    placed = (
        P("panel", None, "front"),
        P("panel", None, "front"),
        P("panel", "front", None),
        P("panel", "front", None, None),
        P("panel", "front", None, None),
        P("panel", "front", None),
        P("panel", "front"),
    )
    return jax.shard_map(
        functools.partial(body, sizes),
        mesh=mesh,
        in_specs=placed,
        out_specs=(P("panel", None, "front"), P("panel", None, "front")),
        check_vma=False,
    )
```

time: 105 us -> 84.5 us (0.80)
  Pallas kernels: 98.7 us -> 78.5 us
    pallas_call x1, Pallas kernels: 98.7 us -> 78.5 us  [body(): pl.pallas_call(functools.partial(kernel, sizes), out_shape=(jax.ShapeDtyp...]
    unnamed x7 -> x10, local copies, waits for them, and re-layouts: 4.65 us -> 5.14 us
where the time goes in v2:
time: 84.5 us; the launch traced here: 84.3 us
  Pallas kernels  78.5 us (93%)
  local copies, waits for them, and re-layouts  5.14 us (6%)
    pallas_call x1, Pallas kernels, body(): pl.pallas_call(functools.partial(kernel, sizes), out_shape=(jax.ShapeDtyp...  78.5 us
    unnamed x10, local copies, waits for them, and re-layouts  5.14 us

profile of v2, /device:TPU:1, one launch (start us, length us, event | category | flops | bytes accessed | tf_op | source)
XLA Modules:
  0.0 84.3 jit_solution(4195152317193268142)
XLA Ops:
  0.6 0.0 copy-start
  0.6 1.0 %copy-done = bf16[1,64,4096]{2,1,0:T(8,128)(2,1)S(1)} copy-done((bf16[1,64,4096]{2,1,0:T(8,128)(2,1)S(1)}, bf16[1,64,4096]{2,1,0:T(8,128)(2,1)}, u32[]{:S(2)}) %copy-start) | copy-done | bytes 524312
  1.7 0.0 copy-start.1
  1.7 0.7 copy-done.1
  2.4 0.0 copy-start.2
  2.4 0.7 copy-done.2
  3.1 0.0 copy-start.3
  3.1 0.7 copy-done.3
  3.8 78.5 %shard_map.86 = (bf16[1,64,128]{2,1,0:T(8,128)(2,1)S(1)}, bf16[1,128,9216]{2,1,0:T(8,128)(2,1)S(1)}) custom-call(bf16[1,64,128]{2,1,0:T(8,128)(2,1)S(1)} %bitcast.4, bf16[1,128,9216]{2,1,0:T(8,128)(2,1)} %ls_hbm.1, bf16[1,64,4096]{2,1,0:T(8,128)(2,1)S(1)} %copy-done, bf16[1,36,256,256]{3,2,1,0:T(8,128)(2,1)} %li_hbm.1, bf16[1,36,128,256]{3,2,1,0:T(8,128)(2,1)} %bd_hbm.1, ...), custom_call_target="tpu_custom_call" | custom-call | tf_op jit(solution)/shard_map/pallas_call | solution.py:414
  82.3 0.6 copy.11
  82.9 1.4 %copy.12 = bf16[1,128,9216]{2,1,0:T(8,128)(2,1)} copy(bf16[1,128,9216]{2,1,0:T(8,128)(2,1)S(1)} %get-tuple-element.9) | data formatting | bytes 4718592
Async XLA Ops:
  0.6 1.0 %copy-start = (bf16[1,64,4096]{2,1,0:T(8,128)(2,1)S(1)}, bf16[1,64,4096]{2,1,0:T(8,128)(2,1)}, u32[]{:S(2)}) copy-start(bf16[1,64,4096]{2,1,0:T(8,128)(2,1)} %ti_hbm.1) | copy-start | bytes 1572868
  1.7 0.7 copy-start.1
  2.4 0.7 copy-start.2
  3.1 0.7 copy-start.3

commit v3 on v2

--- a/solution.py
+++ b/solution.py
@@ -25,10 +25,10 @@
     ts_hbm, ls_hbm, ti_hbm, li_hbm, bd_hbm, tr_hbm, cp_hbm,
     tf_hbm, lf_hbm,
     ts, vec, inv, bnd, rows, cpl,
-    inner, lift, acc, main, halo, main_in, halo_in, tops, gath, tabs, field, own_w, nb_w, half,
+    inner, lift, acc, main, halo, main_in, halo_in, scale, scale_in, tops, gath, tabs, field, own_w, nb_w, half,
     in_sem, small_sem, out_sem,
     ta_send, ta_recv, tc_send, tc_recv,
-    pm_send, pm_recv, ph_send, ph_recv,
+    pm_send, pm_recv, ph_send, ph_recv, pc_send, pc_recv,
     g_send, g_recv, o_send, o_recv,
 ):
     ny, nz, chunks, per = sizes
@@ -131,7 +131,7 @@
             spread = dot(hot_rows(j), bnd[j], NN).astype(BF)
             lift[:, columns_of(j)] = dot(spread, inv[j], NT).astype(BF)
 
-    early = chunks // 3
+    early = 1
     lax.fori_loop(0, early, leaves, 0)
     pl.semaphore_wait(barrier, len(peers))
 
@@ -157,30 +157,40 @@
         share(0, r, 0, 64), share(1, left, 0), share(2, right, 32), share(3, left, 32),
         share(4, right, 0), share(5, far, 0), share(6, far, 32),
     ]
+    small[2].wait()
+    own_scale = cpl[...]
+    blank = jnp.zeros_like(own_scale)
+    own_scale = jnp.concatenate(
+        [jnp.where(c == 0, own_scale, blank), jnp.where(c == 0, blank, own_scale)], axis=1
+    )
+    scale[...] = jnp.broadcast_to(own_scale, scale.shape)
+    scale_in[r, c] = scale[...]
+    scale_sends = []
+    for dq in range(panels):
+        q = lax.rem(r + dq, panels)
+        for n, core in enumerate((c, other)):
+            if dq or n:
+                scale_sends.append(remote(
+                    scale, scale_in.at[r, c], pc_send.at[dq * 2 + n], pc_recv.at[r, c], dev(q, m, core)
+                ))
+    for copy in scale_sends:
+        copy.start()
     first_right.start()
     first_left.start()
     shares[0].start()
 
     lax.fori_loop(early, chunks, leaves, 0)
 
-    for k in (0, 2):
-        small[k].wait()
+    small[0].wait()
     known = -acc[:, :128]
     local = ts[...].astype(F32)
     zero = jnp.zeros_like(local)
     lower = jnp.where(c == 0, local, zero)
     upper = jnp.where(c == 0, zero, local)
     known = known + jnp.transpose(jnp.concatenate([lower, upper], axis=0))
-    scale = cpl[...]
-    blank = jnp.zeros_like(scale)
-    scale = jnp.concatenate(
-        [jnp.where(c == 0, scale, blank), jnp.where(c == 0, blank, scale)], axis=1
-    )
-    scale = jnp.broadcast_to(scale, (8, 128))
     for k in range(8):
-        main[k, :GROUP] = known[k * GROUP : (k + 1) * GROUP]
-        main[k, GROUP:] = scale
-        halo[k] = -acc[k * GROUP : (k + 1) * GROUP, 128:]
+        main[k] = known[k * GROUP : (k + 1) * GROUP].astype(BF)
+        halo[k] = (-acc[k * GROUP : (k + 1) * GROUP, 128:]).astype(BF)
     mine = r * 2 + c
     main_in[r, c] = main[mine]
 
@@ -255,16 +265,18 @@
 
     def meet_pieces(p):
         for core in (0, 1):
-            arrival = remote(main.at[0], main_in.at[p, core], pm_send.at[0], pm_recv.at[p, core], dev(r, m, other))
+            for_main = remote(main.at[0], main_in.at[p, core], pm_send.at[0], pm_recv.at[p, core], dev(r, m, other))
+            for_scale = remote(scale, scale_in.at[p, core], pc_send.at[0], pc_recv.at[p, core], dev(r, m, other))
 
             @pl.when(jnp.logical_or(p != r, c != core))
             def _():
-                arrival.wait_recv()
+                for_scale.wait_recv()
+                for_main.wait_recv()
 
             remote(halo.at[0], halo_in.at[p, core], ph_send.at[0], ph_recv.at[p, core], dev(r, m, other)).wait_recv()
-        a, b = main_in[p, 0], main_in[p, 1]
-        tabs[p] = a[:GROUP] + b[:GROUP] + halo_in[p, 0] + halo_in[p, 1]
-        pair = a[GROUP:] + b[GROUP:]
+        terms = [ref[p, core].astype(F32) for ref in (main_in, halo_in) for core in (0, 1)]
+        tabs[p] = (terms[0] + terms[1]) + (terms[2] + terms[3])
+        pair = scale_in[p, 0] + scale_in[p, 1]
         tabs[4 + p] = jnp.concatenate([pair, pair], axis=0)
 
     def sends(t, s):
@@ -287,14 +299,16 @@
             copy.start()
         meanwhile()
         total = jnp.zeros((GROUP, 128), F32)
-        for dy in sorted(range(ny), key=lambda d: min(d, ny - d)):
-            row = lax.rem(y + dy, ny)
-            for dz in range(nz):
-                if dy or dz:
-                    arrived(t, s, row * nz + lax.rem(z + dz, nz))
-            x = jnp.concatenate([gath[t, row * nz + i] for i in range(nz)], axis=1)
-            cols = pl.ds(pl.multiple_of(row * (nz * 128), nz * 128), nz * 128)
-            total += dot(x, tops[p, :, cols], NT)
+        nearest = [(0, 0)] + steps_away[::-1]
+        cuts = sorted({0} | {len(nearest) * k // 16 for k in (4, 8, 12, 15, 16)})
+        for low, high in zip(cuts, cuts[1:]):
+            tiles = [chip_at(dy, dz) for dy, dz in nearest[low:high]]
+            for n, tile in enumerate(tiles):
+                if low + n:
+                    arrived(t, s, tile)
+            x = jnp.concatenate([gath[t, tile] for tile in tiles], axis=1)
+            w = [tops[p, :, pl.ds(pl.multiple_of(tile * 128, 128), 128)] for tile in tiles]
+            total += dot(x, jnp.concatenate(w, axis=1), NT)
         return total
 
     def send_field(p, value):
@@ -367,7 +381,7 @@
     lax.fori_loop(4, STEPS, backward, 0)
     wait_sends(STEPS - 1, (STEPS - 1) % 2)
     crossed = [first_right, first_left, second_right, second_left, on_right, on_left]
-    for copy in piece_sends + crossed + shares:
+    for copy in scale_sends + piece_sends + crossed + shares:
         copy.wait_send()
 
     for k in range(8):
@@ -411,6 +425,13 @@
     hbm_spec = pl.BlockSpec(memory_space=pltpu.HBM)
     dma = pltpu.SemaphoreType.DMA
     vmem = pltpu.VMEM
+    operands = [
+        pltpu.with_memory_space_constraint(x, pltpu.HBM)
+        for x in (
+            jnp.swapaxes(top_source, 1, 2), leaf_source, top_inverse, leaf_inverse, boundary,
+            jnp.swapaxes(touch_rows, 0, 1), coupling,
+        )
+    ]
     top, leaf = pl.pallas_call(
         functools.partial(kernel, sizes),
         out_shape=(
@@ -429,10 +450,12 @@
             vmem((128, columns), BF),
             vmem((256, columns), BF),
             vmem((128, 256), F32),
-            vmem((8, GROUP + 8, 128), F32),
-            vmem((8, GROUP, 128), F32),
-            vmem((4, 2, GROUP + 8, 128), F32),
-            vmem((4, 2, GROUP, 128), F32),
+            vmem((8, GROUP, 128), BF),
+            vmem((8, GROUP, 128), BF),
+            vmem((4, 2, GROUP, 128), BF),
+            vmem((4, 2, GROUP, 128), BF),
+            vmem((8, 128), F32),
+            vmem((4, 2, 8, 128), F32),
             vmem((4, 128, order), BF),
             vmem((STEPS, ny * nz, GROUP, 128), BF),
             vmem((16, GROUP, 128), F32),
@@ -442,17 +465,14 @@
             vmem((64, 128), BF),
             dma((3, chunks)), dma((4,)), dma((chunks + 1,)),
             dma((6,)), dma((6,)), dma((7,)), dma((7,)),
-            dma((8,)), dma((4, 2)), dma((8,)), dma((4, 2)),
+            dma((8,)), dma((4, 2)), dma((8,)), dma((4, 2)), dma((8,)), dma((4, 2)),
             dma((2, ny * nz - 1)), dma((2, ny * nz)),
             dma((4, 4)), dma((8, 2)),
         ],
         compiler_params=pltpu.CompilerParams(
             collective_id=0, has_side_effects=True, vmem_limit_bytes=50 * 1024 * 1024
         ),
-    )(
-        jnp.swapaxes(top_source, 1, 2), leaf_source, top_inverse, leaf_inverse, boundary,
-        jnp.swapaxes(touch_rows, 0, 1), coupling,
-    )
+    )(*operands)
     return jnp.swapaxes(top, 1, 2), leaf
 
 

time: 84.5 us -> 81.4 us (0.963)
  local copies, waits for them, and re-layouts: 5.14 us -> 2.01 us
    unnamed x10 -> x2, local copies, waits for them, and re-layouts: 5.14 us -> 2.01 us
where the time goes in v3:
time: 81.4 us; the launch traced here: 81.3 us
  Pallas kernels  78.7 us (97%)
  local copies, waits for them, and re-layouts  2.01 us (2%)
    pallas_call x1, Pallas kernels, body(): pl.pallas_call(functools.partial(kernel, sizes), out_shape=(jax.ShapeDtyp...  78.7 us
    unnamed x2, local copies, waits for them, and re-layouts  2.01 us

profile of v3, /device:TPU:1, one launch (start us, length us, event | category | flops | bytes accessed | tf_op | source)
XLA Modules:
  0.0 81.3 jit_solution(2741693258178486811)
XLA Ops:
  0.6 78.7 %shard_map.86 = (bf16[1,64,128]{2,1,0:T(8,128)(2,1)S(1)}, bf16[1,128,9216]{2,1,0:T(8,128)(2,1)S(1)}) custom-call(bf16[1,64,128]{2,1,0:T(8,128)(2,1)} %bitcast.5, bf16[1,128,9216]{2,1,0:T(8,128)(2,1)} %ls_hbm.1, bf16[1,64,4096]{2,1,0:T(8,128)(2,1)} %ti_hbm.1, bf16[1,36,256,256]{3,2,1,0:T(8,128)(2,1)} %li_hbm.1, bf16[1,36,128,256]{3,2,1,0:T(8,128)(2,1)} %bd_hbm.1, ...), custom_call_target="tpu_custom_call" | custom-call | tf_op jit(solution)/shard_map/pallas_call | solution.py:435
  79.3 0.6 copy.11
  79.9 1.4 %copy.12 = bf16[1,128,9216]{2,1,0:T(8,128)(2,1)} copy(bf16[1,128,9216]{2,1,0:T(8,128)(2,1)S(1)} %get-tuple-element.9) | data formatting | bytes 4718592

commit v4 on v3

--- a/solution.py
+++ b/solution.py
@@ -23,10 +23,10 @@
 def kernel(
     sizes,
     ts_hbm, ls_hbm, ti_hbm, li_hbm, bd_hbm, tr_hbm, cp_hbm,
-    tf_hbm, lf_hbm,
+    tf_out, lf_out,
     ts, vec, inv, bnd, rows, cpl,
-    inner, lift, acc, main, halo, main_in, halo_in, scale, scale_in, tops, gath, tabs, field, own_w, nb_w, half,
-    in_sem, small_sem, out_sem,
+    inner, lift, acc, main, halo, main_in, halo_in, scale, scale_in, tops, gath, tabs, field, own_w, nb_w,
+    in_sem, small_sem,
     ta_send, ta_recv, tc_send, tc_recv,
     pm_send, pm_recv, ph_send, ph_recv, pc_send, pc_recv,
     g_send, g_recv, o_send, o_recv,
@@ -401,18 +401,10 @@
     own = own_w[...].reshape(128, 128)
     window = jnp.concatenate([own, nb_w[...].reshape(128, 128)], axis=1)
     turned = jnp.transpose(own.astype(F32))
-    half[...] = jnp.where(c == 0, turned[:64], turned[64:]).astype(BF)
-    top_out = pltpu.make_async_copy(half, tf_hbm.at[0], out_sem.at[chunks])
-    top_out.start()
-    outs = []
+    tf_out[0] = jnp.where(c == 0, turned[:64], turned[64:]).astype(BF)
     for g in range(chunks):
         cols = slice(g * per * width, (g + 1) * per * width)
-        vec[:, cols] = (inner[:, cols].astype(F32) - dot(window, lift[:, cols], NN)).astype(BF)
-        outs.append(pltpu.make_async_copy(vec.at[:, cols], lf_hbm.at[0, :, cols], out_sem.at[g]))
-        outs[-1].start()
-    for copy in outs:
-        copy.wait()
-    top_out.wait()
+        lf_out[0, :, cols] = (inner[:, cols].astype(F32) - dot(window, lift[:, cols], NN)).astype(BF)
 
 
 def body(sizes, top_source, leaf_source, top_inverse, leaf_inverse, boundary, touch_rows, coupling):
@@ -421,7 +413,6 @@
     reach = boundary.shape[2]
     columns = leaves * width
     order = ny * nz * 128
-    any_spec = pl.BlockSpec(memory_space=pl.ANY)
     hbm_spec = pl.BlockSpec(memory_space=pltpu.HBM)
     dma = pltpu.SemaphoreType.DMA
     vmem = pltpu.VMEM
@@ -439,7 +430,7 @@
             jax.ShapeDtypeStruct(leaf_source.shape, BF),
         ),
         in_specs=[hbm_spec] * 7,
-        out_specs=(any_spec, any_spec),
+        out_specs=(pl.BlockSpec(memory_space=pltpu.VMEM),) * 2,
         scratch_shapes=[
             vmem((64, 128), BF),
             vmem((128, columns), BF),
@@ -462,8 +453,7 @@
             vmem((4, GROUP, 128), BF),
             vmem((8, GROUP, 128), BF),
             vmem((8, GROUP, 128), BF),
-            vmem((64, 128), BF),
-            dma((3, chunks)), dma((4,)), dma((chunks + 1,)),
+            dma((3, chunks)), dma((4,)),
             dma((6,)), dma((6,)), dma((7,)), dma((7,)),
             dma((8,)), dma((4, 2)), dma((8,)), dma((4, 2)), dma((8,)), dma((4, 2)),
             dma((2, ny * nz - 1)), dma((2, ny * nz)),

time: 81.4 us -> 80.1 us (0.984)
  Pallas kernels: 78.7 us -> 77.4 us
    pallas_call x1, Pallas kernels: 78.7 us -> 77.4 us  [body(): pl.pallas_call(functools.partial(kernel, sizes), out_shape=(jax.ShapeDtyp...]
where the time goes in v4:
time: 80.1 us
  Pallas kernels  77.4 us (97%)
  local copies, waits for them, and re-layouts  2.01 us (3%)
    pallas_call x1, Pallas kernels, body(): pl.pallas_call(functools.partial(kernel, sizes), out_shape=(jax.ShapeDtyp...  77.4 us
    unnamed x2, local copies, waits for them, and re-layouts  2.01 us

profile of v4, /device:TPU:1, one launch (start us, length us, event | category | flops | bytes accessed | tf_op | source)
XLA Modules:
  0.0 80.1 jit_solution(703246072552873739)
XLA Ops:
  0.6 77.4 %shard_map.86 = (bf16[1,64,128]{2,1,0:T(8,128)(2,1)S(1)}, bf16[1,128,9216]{2,1,0:T(8,128)(2,1)S(1)}) custom-call(bf16[1,64,128]{2,1,0:T(8,128)(2,1)} %bitcast.5, bf16[1,128,9216]{2,1,0:T(8,128)(2,1)} %ls_hbm.1, bf16[1,64,4096]{2,1,0:T(8,128)(2,1)} %ti_hbm.1, bf16[1,36,256,256]{3,2,1,0:T(8,128)(2,1)} %li_hbm.1, bf16[1,36,128,256]{3,2,1,0:T(8,128)(2,1)} %bd_hbm.1, ...), custom_call_target="tpu_custom_call" | custom-call | tf_op jit(solution)/shard_map/pallas_call | solution.py:426
  78.0 0.6 copy.11
  78.7 1.4 %copy.12 = bf16[1,128,9216]{2,1,0:T(8,128)(2,1)} copy(bf16[1,128,9216]{2,1,0:T(8,128)(2,1)S(1)} %get-tuple-element.9) | data formatting | bytes 4718592

commit v5 on v4

--- a/solution.py
+++ b/solution.py
@@ -195,17 +195,17 @@
     main_in[r, c] = main[mine]
 
     piece_sends = []
-    for dq in range(panels):
+    for dq in (2, 1, 3, 0):
         q = lax.rem(r + dq, panels)
         for n, core in enumerate((c, other)):
             k, slot = q * 2 + core, dq * 2 + n
+            piece_sends.append(remote(
+                halo.at[k], halo_in.at[r, c], ph_send.at[slot], ph_recv.at[r, c], dev(q, side, core)
+            ))
             if slot:
                 piece_sends.append(remote(
                     main.at[k], main_in.at[r, c], pm_send.at[slot], pm_recv.at[r, c], dev(q, m, core)
                 ))
-            piece_sends.append(remote(
-                halo.at[k], halo_in.at[r, c], ph_send.at[slot], ph_recv.at[r, c], dev(q, side, core)
-            ))
     for copy in piece_sends:
         copy.start()
 
@@ -329,15 +329,14 @@
     def field_copies(p):
         mine = r * 2 + c
         return [
-            remote(field.at[p], own_w.at[mine], o_send.at[p, 1], o_recv.at[mine, 0], dev(p, m, other)),
             remote(field.at[p], nb_w.at[mine], o_send.at[p, 2], o_recv.at[mine, 1], dev(p, down, 1)),
             remote(field.at[p], nb_w.at[mine], o_send.at[p, 3], o_recv.at[mine, 1], dev(p, up, 0)),
+            remote(field.at[p], own_w.at[mine], o_send.at[p, 1], o_recv.at[mine, 0], dev(p, m, other)),
         ]
 
     tabs[12] = jnp.zeros((GROUP, 128), F32)
 
     def forward(t, carry):
-        meet_pieces(t)
         value = (tabs[t] + tabs[4 + t] * tabs[12]).astype(BF)
 
         def meanwhile():
@@ -348,11 +347,16 @@
             lifts(t)
             meet_tops(t)
 
+            @pl.when(t < panels - 1)
+            def _():
+                meet_pieces(t + 1)
+
         top = solve(t, t, value, meanwhile).astype(BF).astype(F32)
         tabs[8 + t] = top
         tabs[12] = top
         return carry
 
+    meet_pieces(0)
     lax.fori_loop(0, panels, forward, 0)
 
     nothing = jnp.zeros((GROUP, chips * 128), BF)
@@ -384,20 +388,20 @@
     for copy in scale_sends + piece_sends + crossed + shares:
         copy.wait_send()
 
+    for p in range(panels):
+        @pl.when(p != r)
+        def _():
+            remote(field.at[p], own_w.at[0], o_send.at[p, 0], o_recv.at[0, 0], dev(r, m, other)).wait_send()
+
+        for copy in field_copies(p):
+            copy.wait_send()
+
     for k in range(8):
         @pl.when(k != r * 2 + c)
         def _():
             remote(field.at[0], own_w.at[k], o_send.at[0, 0], o_recv.at[k, 0], dev(r, m, other)).wait_recv()
 
         remote(field.at[0], nb_w.at[k], o_send.at[0, 0], o_recv.at[k, 1], dev(r, m, other)).wait_recv()
-    for p in range(panels):
-        @pl.when(p != r)
-        def _():
-            remote(field.at[p], own_w.at[0], o_send.at[p, 0], o_recv.at[0, 0], dev(r, m, other)).wait_send()
-
-        for copy in field_copies(p):
-            copy.wait_send()
-
     own = own_w[...].reshape(128, 128)
     window = jnp.concatenate([own, nb_w[...].reshape(128, 128)], axis=1)
     turned = jnp.transpose(own.astype(F32))

time: 80.1 us -> 80.1 us (level)
  no operation moved by 1% of the time
where the time goes in v5:
time: 80.1 us; the launch traced here: 80 us
  Pallas kernels  77.3 us (97%)
  local copies, waits for them, and re-layouts  2.01 us (3%)
    pallas_call x1, Pallas kernels, body(): pl.pallas_call(functools.partial(kernel, sizes), out_shape=(jax.ShapeDtyp...  77.3 us
    unnamed x2, local copies, waits for them, and re-layouts  2.01 us

profile of v5, /device:TPU:1, one launch (start us, length us, event | category | flops | bytes accessed | tf_op | source)
XLA Modules:
  0.0 80.0 jit_solution(1248670763624825607)
XLA Ops:
  0.6 77.3 %shard_map.86 = (bf16[1,64,128]{2,1,0:T(8,128)(2,1)S(1)}, bf16[1,128,9216]{2,1,0:T(8,128)(2,1)S(1)}) custom-call(bf16[1,64,128]{2,1,0:T(8,128)(2,1)} %bitcast.5, bf16[1,128,9216]{2,1,0:T(8,128)(2,1)} %ls_hbm.1, bf16[1,64,4096]{2,1,0:T(8,128)(2,1)} %ti_hbm.1, bf16[1,36,256,256]{3,2,1,0:T(8,128)(2,1)} %li_hbm.1, bf16[1,36,128,256]{3,2,1,0:T(8,128)(2,1)} %bd_hbm.1, ...), custom_call_target="tpu_custom_call" | custom-call | tf_op jit(solution)/shard_map/pallas_call | solution.py:430
  78.0 0.6 copy.11
  78.6 1.4 %copy.12 = bf16[1,128,9216]{2,1,0:T(8,128)(2,1)} copy(bf16[1,128,9216]{2,1,0:T(8,128)(2,1)S(1)} %get-tuple-element.9) | data formatting | bytes 4718592
